TPU v7x, 256 devices: a whole 4x4x8 slice. The times are simulated.
256 devices in a mesh: seq: 32 (over y_hi, z, core), head: 8 (over x, y_lo).
Axes of the slice: x: 4, y: 4 (y_hi: 2, y_lo: 2; y = y_hi * 2 + y_lo), z: 8, core: 2. Of those that a mesh axis runs over, the one named last changes fastest.
Arguments:
- queries: bfloat16 [49152, 4096], P('seq', 'head'), may hold values from -6 to 6, as said below
- keys: bfloat16 [49152, 2048], P('seq', 'head'), may hold values from -6 to 6
- values: bfloat16 [49152, 2048], P('seq', 'head'), may hold values from -6 to 6
- q_gain: float32 [128], replicated, may hold values from -0.5 to 5
- k_gain: float32 [128], replicated, may hold values from -0.5 to 5
- positions: int32 [49152], P('seq'), may hold values from 2048 to 52222, as said below
- prefix_cache: bfloat16 [32, 2048, 4096], P('seq', 'head'), may hold values from -6 to 6
- owner: int32 [1], replicated, may hold values from 0 to 31
Outputs:
- attended: bfloat16 [49152, 4096], P('seq', 'head')
Inputs may be any that keep to these rules, and one draw needn't show every extreme that they name: queries and keys are of order one. positions[i] = positions[0] + i, and positions[0] is 2048 or more and under 2048 + 1024.
All inputs are finite; a program needn't handle non-finite values.
Results may differ from a plain program's by a relative error of at most 0.02.
Values may be sent and summed in bfloat16 or wider, within the bound.
No kernel may reach another device: no remote copies, remote signals or barrier semaphores. Data moves between devices by JAX's collectives and lax.ppermute only.
A program may use at most 128 MiB of HBM per device.

v0:
```python
import functools

import jax
import jax.numpy as jnp
from jax import lax
from jax.experimental import pallas as pl
from jax.experimental.pallas import tpu as pltpu
from jax.sharding import Mesh, PartitionSpec as P

HD = 128
WINDOW = 1024
QSCALAR = 168
YH, NZ, NC, NH = 2, 8, 2, 8
SEQ = ("yh", "z", "core")
BAND_TILE = 256
TILE = 512
CHUNK = 256
NEG = -1e30
BIG = 1e30
VMEM_LIMIT = 24 * 1024 * 1024


def swapped(array, axis):
    return lax.ppermute(array, axis, [(0, 1), (1, 0)])


def round_z(array, r):
    return lax.ppermute(array, "z", [(i, (i + r) % NZ) for i in range(NZ)])


def pick(array, at):
    return lax.dynamic_index_in_dim(array, at, 0, keepdims=False)


def halved(part, axis, root_at):
    at = lax.axis_index(axis)
    part = part.reshape(2, part.shape[0] // 2, part.shape[1])
    came = swapped(pick(part, 1 - at), axis)
    return jnp.where(root_at == at, pick(part, at), came)


def tables(cos_ref, sin_ref, at, gain, scale):
    cosine, sine = cos_ref[at, :], sin_ref[at, :]
    cosine = jnp.concatenate([cosine, cosine], axis=1)
    sine = jnp.concatenate([-sine, sine], axis=1)
    return cosine * (gain * scale), sine * (pltpu.roll(gain, HD // 2, 1) * scale)


def normed(rows, direct, crossed):
    wide = rows.astype(jnp.float32)
    square = wide * wide
    high = square.astype(jnp.bfloat16)
    low = (square - high.astype(jnp.float32)).astype(jnp.bfloat16)
    even = jnp.full((HD, HD), 1.0 / HD, jnp.bfloat16)
    mean_sq = jnp.dot(high, even, preferred_element_type=jnp.float32)
    mean_sq = mean_sq + jnp.dot(low, even, preferred_element_type=jnp.float32)
    other = pltpu.roll(rows, HD // 2, 1).astype(jnp.float32)
    return ((wide * direct + other * crossed) * lax.rsqrt(mean_sq + 1e-06)).astype(jnp.bfloat16)


def dot_t(a, b):
    return lax.dot_general(a, b, (((1,), (1,)), ((), ())), preferred_element_type=jnp.float32)


def rows_at(t, tile):
    return pl.ds(pl.multiple_of(t * tile, tile), tile)


def columns_of(h):
    return slice(h * HD, (h + 1) * HD)


def stacked(ref, at, heads):
    return jnp.concatenate([ref[at, columns_of(h)] for h in heads], axis=0)


def prep_kernel(q_ref, k_ref, qg_ref, kg_ref, cos_ref, sin_ref, qn_ref, kn_ref):
    def own(t, _):
        at = rows_at(t, BAND_TILE)
        at_table = rows_at(t + WINDOW // BAND_TILE, BAND_TILE)
        q_tables = tables(cos_ref, sin_ref, at_table, qg_ref[...], QSCALAR ** (-0.5))
        k_tables = tables(cos_ref, sin_ref, at_table, kg_ref[...], 1.0)
        for c in range(k_ref.shape[1] // HD):
            kn_ref[at, columns_of(c)] = normed(k_ref[at, columns_of(c)], *k_tables)
        for h in range(q_ref.shape[1] // HD):
            qn_ref[at, columns_of(h)] = normed(q_ref[at, columns_of(h)], *q_tables)
        return 0

    lax.fori_loop(0, q_ref.shape[0] // BAND_TILE, own, 0)


def halo_kernel(k_ref, kg_ref, cos_ref, sin_ref, kn_ref):
    def one(t, _):
        at = rows_at(t, BAND_TILE)
        k_tables = tables(cos_ref, sin_ref, at, kg_ref[...], 1.0)
        for c in range(kn_ref.shape[1] // HD):
            kn_ref[at, columns_of(c)] = normed(k_ref[at, columns_of(c)], *k_tables)
        return 0

    lax.fori_loop(0, WINDOW // BAND_TILE, one, 0)


def attend(state, query, key, value, keep_score=None, dead=None):
    score = dot_t(query, key)
    if keep_score is not None:
        score = jnp.where(keep_score, score, NEG)
    top = jnp.max(score, axis=1, keepdims=True)
    if dead is not None:
        top = jnp.where(dead, NEG, top)
    top = jnp.broadcast_to(top, query.shape)
    if state is not None:
        top = jnp.maximum(state[0], top)
    minus = top if dead is None else jnp.where(dead, BIG, top)
    weight = jnp.concatenate(
        [jnp.exp(score[:, i : i + HD] - minus).astype(jnp.bfloat16) for i in range(0, score.shape[1], HD)],
        axis=1,
    )
    value = jnp.concatenate([value, jnp.ones_like(value)], axis=1)
    out = jnp.dot(weight, value, preferred_element_type=jnp.float32)
    summed, total = out[:, :HD], out[:, HD:]
    if state is not None:
        keep = jnp.exp(state[0] - top)
        summed, total = state[1] * keep + summed, state[2] * keep + total
    return top, summed, total


def band_kernel(part, halo_rows, first_ref, q_ref, k_ref, v_ref, *rest):
    kb_ref, vb_ref = rest[:2] if halo_rows else (None, None)
    outs = rest[-3:]
    kv = k_ref.shape[1] // HD
    group = q_ref.shape[1] // HD // kv
    rows_in = lax.broadcasted_iota(jnp.int32, (group * BAND_TILE, CHUNK), 0) % BAND_TILE
    columns_in = lax.broadcasted_iota(jnp.int32, (group * BAND_TILE, CHUNK), 1)
    early = columns_in > rows_in
    late = columns_in <= rows_in
    reach = WINDOW // CHUNK
    is_first = first_ref[0] == 1
    tiles = q_ref.shape[0] // BAND_TILE
    for t in range(tiles):
        at = slice(t * BAND_TILE, (t + 1) * BAND_TILE)
        queries = [stacked(q_ref, at, range(c * group, (c + 1) * group)) for c in range(kv)]
        state = [None] * kv
        for j in range(reach, -1, -1):
            e = part * tiles + t + j - reach
            mine = e >= 0
            start = e * CHUNK if mine else halo_rows + e * CHUNK
            keys_at = slice(start, start + CHUNK)
            for c in range(kv):
                state[c] = attend(
                    state[c],
                    queries[c],
                    (k_ref if mine else kb_ref)[keys_at, columns_of(c)],
                    (v_ref if mine else vb_ref)[keys_at, columns_of(c)],
                    keep_score=late if j == reach else early if j == 0 else None,
                    dead=None if mine else is_first,
                )
        for c in range(kv):
            for g in range(group):
                rows = slice(g * BAND_TILE, (g + 1) * BAND_TILE)
                for ref, value in zip(outs, state[c]):
                    ref[at, columns_of(c * group + g)] = value[rows]


def blocks_of(p_refs):
    blocks, held, room = [], [], CHUNK
    for p_ref in p_refs:
        start = 0
        while start < p_ref.shape[0]:
            rows = min(room, p_ref.shape[0] - start)
            held.append((p_ref, start, rows))
            start, room = start + rows, room - rows
            if room == 0:
                blocks.append(held)
                held, room = [], CHUNK
    if held and blocks and CHUNK - room < CHUNK:
        blocks[-1] = blocks[-1] + held
    elif held:
        blocks.append(held)
    return blocks


def joined(block, h):
    parts = [p_ref[start : start + rows, columns_of(h)] for p_ref, start, rows in block]
    return parts[0] if len(parts) == 1 else jnp.concatenate(parts, axis=0)


def prefix_kernel(last, bands, pieces, q_ref, *rest):
    states, rest = [rest[3 * i : 3 * i + 3] for i in range(bands)], rest[3 * bands :]
    p_refs, outs = rest[:pieces], rest[pieces:]
    kv = p_refs[0].shape[1] // (2 * HD)
    group = q_ref.shape[1] // HD // kv
    each = states[0][0].shape[0]

    def step(t, state_refs, at_in):
        at = rows_at(t, TILE)
        heads = [range(c * group, (c + 1) * group) for c in range(kv)]
        queries = [stacked(q_ref, at, heads[c]) for c in range(kv)]
        state = [tuple(stacked(ref, at_in, heads[c]) for ref in state_refs) for c in range(kv)]
        for block in blocks_of(p_refs):
            for c in range(kv):
                state[c] = attend(state[c], queries[c], joined(block, 2 * c), joined(block, 2 * c + 1))
        for c in range(kv):
            result = [(state[c][1] / state[c][2]).astype(jnp.bfloat16)] if last else state[c]
            for g in range(group):
                rows = slice(g * TILE, (g + 1) * TILE)
                for ref, part in zip(outs, result):
                    ref[at, columns_of(c * group + g)] = part[rows]

    if bands > 1:
        for i in range(q_ref.shape[0] // TILE):
            step(i, states[i * TILE // each], slice(i * TILE % each, i * TILE % each + TILE))
    else:

        def one(t, _):
            step(t, states[0], rows_at(t, TILE))
            return 0

        lax.fori_loop(0, q_ref.shape[0] // TILE, one, 0)


WHOLE = pl.BlockSpec(memory_space=pltpu.VMEM)
PARAMS = pltpu.CompilerParams(vmem_limit_bytes=VMEM_LIMIT)


def cost(pairs, in_out):
    return pl.CostEstimate(flops=8 * pairs * HD, transcendentals=pairs, bytes_accessed=in_out)


def normed_part(kernel, outs, *args):
    size = sum(o.size for o in outs)
    return pl.pallas_call(
        kernel,
        out_shape=outs,
        in_specs=[WHOLE] * len(args),
        out_specs=(WHOLE,) * len(outs),
        compiler_params=PARAMS,
        cost_estimate=pl.CostEstimate(flops=60 * size, transcendentals=size // HD, bytes_accessed=6 * size),
        name="norm_rope",
    )(*args)


def band_part(part, parts, first, q, k, v, key_before, before):
    width, wide = q.shape[1], k.shape[1]
    rows = q.shape[0] // parts
    halo_rows = max(0, WINDOW - part * rows)
    own = pl.BlockSpec(((part + 1) * rows, wide), lambda i: (0, 0))
    operands = [first, q, k, v]
    in_specs = [
        pl.BlockSpec(memory_space=pltpu.SMEM),
        pl.BlockSpec((rows, width), lambda i: (part, 0)),
        own,
        own,
    ]
    if halo_rows:
        at = WINDOW // halo_rows - 1
        operands += [key_before, before]
        in_specs += [
            pl.BlockSpec((halo_rows, wide), lambda i: (at, 0)),
            pl.BlockSpec((halo_rows, wide), lambda i: (at, 1)),
        ]
    return pl.pallas_call(
        functools.partial(band_kernel, part, halo_rows),
        grid=(1,),
        out_shape=(jax.ShapeDtypeStruct((rows, width), jnp.float32),) * 3,
        in_specs=in_specs,
        out_specs=(WHOLE,) * 3,
        compiler_params=PARAMS,
        cost_estimate=cost(rows * (width // HD) * (WINDOW + BAND_TILE), 5 << 20),
        name="band",
    )(*operands)


def prefix_part(last, q, states, *pieces):
    local, width = q.shape
    flat = [part for state in states for part in state]
    if last:
        out_shape = jax.ShapeDtypeStruct((local, width), jnp.bfloat16)
        out_specs = WHOLE
    else:
        out_shape = (jax.ShapeDtypeStruct((local, width), jnp.float32),) * 3
        out_specs = (WHOLE,) * 3
    return pl.pallas_call(
        functools.partial(prefix_kernel, last, len(states), len(pieces)),
        out_shape=out_shape,
        in_specs=[WHOLE] * (1 + len(flat) + len(pieces)),
        out_specs=out_specs,
        compiler_params=PARAMS,
        cost_estimate=cost(local * (width // HD) * sum(p.shape[0] for p in pieces), 10 << 20),
        name="prefix_last" if last else "prefix",
    )(q, *flat, *pieces)


def on_device(queries, keys, values, q_gain, k_gain, positions, prefix_cache, owner):
    local = queries.shape[0]
    root = owner[0]
    root_y, root_z, root_c = root // (NZ * NC), (root // NC) % NZ, root % NC
    q_gain, k_gain = (1.0 + q_gain)[None], (1.0 + k_gain)[None]
    first = (lax.axis_index(SEQ) == 0).astype(jnp.int32).reshape(1)

    slab = halved(prefix_cache[0], "core", root_c)
    onward = [(i, i + 1) for i in range(YH * NZ * NC - 1)]
    tail = jnp.concatenate([keys[local - WINDOW :], values[local - WINDOW :]], axis=1)
    slab, tail = lax.optimization_barrier((slab, tail))
    before = lax.ppermute(tail, SEQ, onward)
    slab = halved(slab, "yh", root_y)

    half = HD // 2
    freq = 10000.0 ** (-(jnp.arange(half).astype(jnp.float32) * 2.0) / HD)
    extended = positions[0] + jnp.arange(-WINDOW, local, dtype=jnp.int32)
    angle = extended.astype(jnp.float32)[:, None] * freq[None, :]
    cosine, sine = jnp.cos(angle), jnp.sin(angle)
    query, key = normed_part(
        prep_kernel,
        (
            jax.ShapeDtypeStruct(queries.shape, jnp.bfloat16),
            jax.ShapeDtypeStruct(keys.shape, jnp.bfloat16),
        ),
        queries, keys, q_gain, k_gain, cosine, sine,
    )
    slab, query, before = lax.optimization_barrier((slab, query, before))

    rows, wide = slab.shape
    parts = slab.reshape(NZ, rows // NZ, NH, wide // NH).transpose(0, 2, 1, 3)
    parts = parts.reshape(NZ * NH, rows // NZ, wide // NH)
    parts = lax.all_to_all(parts, ("z", "head"), split_axis=0, concat_axis=0, tiled=True)
    (key_before,) = normed_part(
        halo_kernel,
        (jax.ShapeDtypeStruct((WINDOW, keys.shape[1]), jnp.bfloat16),),
        before, k_gain, cosine, sine,
    )

    def band(part, first):
        return band_part(part, 3, first, query, key, values, key_before, before)

    states = [band(0, first)]
    parts, top = lax.optimization_barrier((parts, states[0][0]))
    states[0] = (top, *states[0][1:])
    mine = pick(parts.reshape(NZ, NH, rows // NZ, wide // NH), root_z)
    mine = mine.reshape(NH * rows // NZ, wide // NH)
    mine, first = lax.optimization_barrier((mine, first))

    far = swapped(mine, "yh")
    states.append(band(1, first))
    far, top = lax.optimization_barrier((far, states[1][0]))
    states[1] = (top, *states[1][1:])
    pair = jnp.concatenate([mine, far], axis=0)
    pair, first = lax.optimization_barrier((pair, first))

    second = [round_z(pair, NZ // 2), round_z(pair, 2), round_z(pair, -2)]
    states.append(band(2, first))
    second, top = lax.optimization_barrier((second, states[2][0]))
    states[2] = (top, *states[2][1:])
    near = jnp.concatenate([pair, *second], axis=0)
    near_sibling = swapped(near, "core")
    double = jnp.concatenate([pair, second[0]], axis=0)
    third = [round_z(double, 1), round_z(double, -1)]
    state = prefix_part(False, query, states, near, near_sibling)
    third, top = lax.optimization_barrier((third, state[0]))
    third = jnp.concatenate(third, axis=0)
    third_sibling = swapped(third, "core")
    state = prefix_part(False, query, [(top, *state[1:])], third)
    return prefix_part(True, query, [state], third_sibling)


def solution(mesh):
    fine = Mesh(mesh.devices.reshape(YH, NZ, NC, NH), SEQ + ("head",))
    return jax.shard_map(
        on_device,
        mesh=fine,
        in_specs=(
            P(SEQ, "head"),
            P(SEQ, "head"),
            P(SEQ, "head"),
            P(),
            P(),
            P(SEQ),
            P(SEQ, "head", None),
            P(),
        ),
        out_specs=P(SEQ, "head"),
        check_vma=False,
    )
```

profile of v0, /device:TPU:1, one launch (start us, length us, event | category | flops | bytes accessed | tf_op | source)
XLA Modules:
  0.0 120.2 jit_solution(1035670605977617850)
XLA Ops:
  0.0 2.4 %dynamic-slice_bitcast_fusion = bf16[128,4096]{1,0:T(8,128)(2,1)} fusion(bf16[2,128,4096]{2,1,0:T(8,128)(2,1)} %bitcast.31, s32[]{:T(128)S(6)} %select_n.57), kind=kLoop, calls=%fused_computation.4 | loop fusion | bytes 2097156 | tf_op jit(solution)/shard_map/jit(dynamic_index_in_dim)/squeeze | solution.py:32
  2.4 3.2 %collective-permute-start = (bf16[128,4096]{1,0:T(8,128)(2,1)}, bf16[128,4096]{1,0:T(8,128)(2,1)}, u32[]{:S(2)}, u32[]{:S(2)}) collective-permute-start(bf16[128,4096]{1,0:T(8,128)(2,1)} %dynamic-slice_bitcast_fusion), channel_id=1, source_target_pairs={{0,8},{8,0},{1,9},{9,1},{2,10},{10,2},{3,11},{11,3},{4,12},{12,4},... | collective-permute-start | bytes 3145736 | tf_op jit(solution)/shard_map/ppermute | solution.py:24
  6.3 1.4 %slice.11 = s32[1]{0:T(128)} slice(s32[1536]{0:T(1024)} %param.13), slice={[0:1]} | slice | bytes 8 | tf_op jit(solution)/shard_map/slice | solution.py:309
  10.8 1.2 collective-permute-start.1
  11.9 4.6 %multiply_sine_fusion = (f32[2560,64]{1,0:T(8,128)S(1)}, f32[2560,64]{1,0:T(8,128)S(1)}) fusion(f32[64]{0:T(128)S(1)} %multiply_power_fusion, f32[2560]{0:T(1024)S(1)} %add_convert_fusion), kind=kLoop, calls=%fused_computation | loop fusion | flops 163840 | bytes 1321216 | tf_op jit(solution)/shard_map/sin | solution.py:311
  16.6 4.9 %collective-permute-start.2 = (bf16[1024,512]{1,0:T(8,128)(2,1)}, bf16[1024,512]{1,0:T(8,128)(2,1)S(1)}, u32[]{:S(2)}, u32[]{:S(2)}) collective-permute-start(bf16[1024,512]{1,0:T(8,128)(2,1)} %pad_maximum_fusion), channel_id=1, source_target_pairs={{0,8},{8,16},{16,24},{24,32},{32,40},{40,48},{48,56},{56,64},{64,7... | collective-permute-start | bytes 3145736 | tf_op jit(solution)/shard_map/ppermute | solution.py:304
  21.6 1.4 %copy-done.4 = bf16[1536,512]{1,0:T(8,128)(2,1)S(1)} copy-done((bf16[1536,512]{1,0:T(8,128)(2,1)S(1)}, bf16[1536,512]{1,0:T(8,128)(2,1)}, u32[]{:S(2)}) %copy-start.4) | copy-done | bytes 1572888
  23.0 2.8 %norm_rope.2 = (bf16[1536,512]{1,0:T(8,128)(2,1)S(1)}, bf16[1536,256]{1,0:T(8,128)(2,1)S(1)}) custom-call(bf16[1536,512]{1,0:T(8,128)(2,1)S(1)} %copy-done.4, bf16[1536,256]{1,0:T(8,128)(2,1)S(1)} %copy-done, f32[1,128]{1,0:T(1,128)S(1)} %add_bitcast_fusion.1.qg_ref, f32[1,128]{1,0:T(1,128)S(1)} %add_bitcast_fusion.kg_ref, ...), custom_call_target="tpu_custom_call" | custom-call | flops 70778880 | bytes 7077888 | tf_op jit(solution)/shard_map/norm_rope/pallas_call | solution.py:231
  26.9 2.2 %bitcast_select_fusion.1 = bf16[64,4096]{1,0:T(8,128)(2,1)} fusion(bf16[64,4096]{1,0:T(8,128)(2,1)} %collective-permute-done.1, bf16[2,64,4096]{2,1,0:T(8,128)(2,1)S(1)} %bitcast.30, s32[]{:T(128)S(6)} %select_n.59, pred[]{:T(512)S(6)} %eq.12), kind=kLoop, calls=%fused_computation.5 | loop fusion | flops 262144 | bytes 1572869 | tf_op jit(solution)/shard_map/jit(_where)/select_n | solution.py:39
  29.1 4.4 %collective-permute-done.2.k_ref.rest_1_ = bf16[1024,512]{1,0:T(8,128)(2,1)S(1)} collective-permute-done((bf16[1024,512]{1,0:T(8,128)(2,1)}, bf16[1024,512]{1,0:T(8,128)(2,1)S(1)}, u32[]{:S(2)}, u32[]{:S(2)}) %collective-permute-start.2) | collective-permute-done | bytes 1048608 | tf_op jit(solution)/shard_map/ppermute | solution.py:304
  34.6 11.4 %all-to-all-start = ((bf16[64,8,512]{2,1,0:T(8,128)(2,1)}), bf16[64,8,512]{2,1,0:T(8,128)(2,1)}, u32[]{:S(2)}, u32[]{:S(2)}) async-start(bf16[64,8,512]{2,1,0:T(8,128)(2,1)} %bitcast.12), calls=%async_computation | async-start | bytes 1048576 | tf_op jit(solution)/shard_map/all_to_all | solution.py:325
  46.0 1.2 %copy-done.6 = bf16[1024,512]{1,0:T(8,128)(2,1)S(1)} copy-done((bf16[1024,512]{1,0:T(8,128)(2,1)S(1)}, bf16[1024,512]{1,0:T(8,128)(2,1)}, u32[]{:S(2)}) %copy-start.6) | copy-done | bytes 1048600
  49.1 4.0 %band.3 = (f32[512,512]{1,0:T(8,128)S(1)}, f32[512,512]{1,0:T(8,128)S(1)}, f32[512,512]{1,0:T(8,128)S(1)}) custom-call(s32[1]{0:T(128)} %bitcast.13.first_ref, bf16[1536,512]{1,0:T(8,128)(2,1)S(1)} %copy-done.2, bf16[1536,256]{1,0:T(8,128)(2,1)S(1)} %copy-done.12, bf16[1536,256]{1,0:T(8,128)(2,1)S(1)} %copy-done.8, bf16[1024,256]{1,0:T(8,128)(2,1)S(1)} %norm_rope.3.rest_0_, ...), custom_call_target="tpu_custom_call" | custom-call | flops 2684354560 | bytes 5242880 | tf_op jit(solution)/shard_map/band/pallas_call | solution.py:261
  56.0 2.9 %all-to-all-done = bf16[64,8,512]{2,1,0:T(8,128)(2,1)} async-done(((bf16[64,8,512]{2,1,0:T(8,128)(2,1)}), bf16[64,8,512]{2,1,0:T(8,128)(2,1)}, u32[]{:S(2)}, u32[]{:S(2)}) %all-to-all-start) | async-done | bytes 524320 | tf_op jit(solution)/shard_map/all_to_all | solution.py:325
  59.7 1.6 %collective-permute-start.3 = (bf16[64,512]{1,0:T(8,128)(2,1)S(1)}, bf16[64,512]{1,0:T(8,128)(2,1)S(1)}, u32[]{:S(2)}, u32[]{:S(2)}) collective-permute-start(bf16[64,512]{1,0:T(8,128)(2,1)S(1)} %dynamic-slice_bitcast_fusion.2), channel_id=1, source_target_pairs={{0,128},{128,0},{1,129},{129,1},{2,130},{130,2},{3,131},{131,3},{4... | collective-permute-start | bytes 196616 | tf_op jit(solution)/shard_map/ppermute | solution.py:24
  63.5 3.7 %band.4 = (f32[512,512]{1,0:T(8,128)S(1)}, f32[512,512]{1,0:T(8,128)S(1)}, f32[512,512]{1,0:T(8,128)S(1)}) custom-call(s32[1]{0:T(128)} %bitcast.13.first_ref, bf16[1536,512]{1,0:T(8,128)(2,1)S(1)} %copy-done.3, bf16[1536,256]{1,0:T(8,128)(2,1)S(1)} %copy-done.13, bf16[1536,256]{1,0:T(8,128)(2,1)S(1)} %copy-done.9, bf16[1024,256]{1,0:T(8,128)(2,1)S(1)} %norm_rope.3.rest_0_, ...), custom_call_target="tpu_custom_call" | custom-call | flops 2684354560 | bytes 5242880 | tf_op jit(solution)/shard_map/band/pallas_call | solution.py:261
  67.3 5.5 %collective-permute-start.4 = (bf16[128,512]{1,0:T(8,128)(2,1)S(1)}, bf16[128,512]{1,0:T(8,128)(2,1)S(1)}, u32[]{:S(2)}, u32[]{:S(2)}) collective-permute-start(bf16[128,512]{1,0:T(8,128)(2,1)S(1)} %pad_maximum_fusion.1), channel_id=1, source_target_pairs={{0,64},{16,80},{32,96},{48,112},{64,0},{80,16},{96,32},{112,48},{1... | collective-permute-start | bytes 393224 | tf_op jit(solution)/shard_map/ppermute | solution.py:28
  73.5 14.8 %collective-permute-start.6 = (bf16[128,512]{1,0:T(8,128)(2,1)S(1)}, bf16[128,512]{1,0:T(8,128)(2,1)S(1)}, u32[]{:S(2)}, u32[]{:S(2)}) collective-permute-start(bf16[128,512]{1,0:T(8,128)(2,1)S(1)} %pad_maximum_fusion.1), channel_id=1, source_target_pairs={{0,96},{16,112},{32,0},{48,16},{64,32},{80,48},{96,64},{112,80},{1... | collective-permute-start | bytes 393224 | tf_op jit(solution)/shard_map/ppermute | solution.py:28
  88.3 3.5 %band.5 = (f32[512,512]{1,0:T(8,128)S(1)}, f32[512,512]{1,0:T(8,128)S(1)}, f32[512,512]{1,0:T(8,128)S(1)}) custom-call(s32[1]{0:T(128)} %bitcast.13.first_ref, bf16[1536,512]{1,0:T(8,128)(2,1)S(1)} %copy-done.3, bf16[1536,256]{1,0:T(8,128)(2,1)S(1)} %copy-done.13, bf16[1536,256]{1,0:T(8,128)(2,1)S(1)} %copy-done.10), custom_call_target="tpu_custom_call" | custom-call | flops 2684354560 | bytes 5242880 | tf_op jit(solution)/shard_map/band/pallas_call | solution.py:261
  91.9 6.0 %collective-permute-start.9 = (bf16[512,512]{1,0:T(8,128)(2,1)S(1)}, bf16[512,512]{1,0:T(8,128)(2,1)S(1)}, u32[]{:S(2)}, u32[]{:S(2)}) collective-permute-start(bf16[512,512]{1,0:T(8,128)(2,1)S(1)} %constant_dynamic-update-slice_fusion.2.rest_9_), channel_id=1, source_target_pairs={{0,8},{8,0},{1,9},{9,1},{2,10},{10,2},{3,11},{11,3},{4,12},{12,4},... | collective-permute-start | bytes 1572872 | tf_op jit(solution)/shard_map/ppermute | solution.py:24
  97.9 2.7 %collective-permute-start.8 = (bf16[256,512]{1,0:T(8,128)(2,1)S(1)}, bf16[256,512]{1,0:T(8,128)(2,1)S(1)}, u32[]{:S(2)}, u32[]{:S(2)}) collective-permute-start(bf16[256,512]{1,0:T(8,128)(2,1)S(1)} %get-tuple-element.80), channel_id=1, source_target_pairs={{0,112},{16,0},{32,16},{48,32},{64,48},{80,64},{96,80},{112,96},{1... | collective-permute-start | bytes 786440 | tf_op jit(solution)/shard_map/ppermute | solution.py:28
  100.6 7.9 %prefix.2 = (f32[1536,512]{1,0:T(8,128)S(1)}, f32[1536,512]{1,0:T(8,128)S(1)}, f32[1536,512]{1,0:T(8,128)S(1)}) custom-call(bf16[1536,512]{1,0:T(8,128)(2,1)S(1)} %copy-done.3, f32[512,512]{1,0:T(8,128)S(1)} %copy-done.15, f32[512,512]{1,0:T(8,128)S(1)} %copy-done.17, f32[512,512]{1,0:T(8,128)S(1)} %copy-done.19, f32[512,512]{1,0:T(8,128)S(1)} %get-tuple-element.62.rest_3_, ...), custom_call_target="tpu_custom_call" | custom-call | flops 6442450944 | bytes 10485760 | tf_op jit(solution)/shard_map/prefix/pallas_call | solution.py:282
  109.3 4.7 %prefix.3 = (f32[1536,512]{1,0:T(8,128)S(1)}, f32[1536,512]{1,0:T(8,128)S(1)}, f32[1536,512]{1,0:T(8,128)S(1)}) custom-call(bf16[1536,512]{1,0:T(8,128)(2,1)S(1)} %copy-done.3, f32[1536,512]{1,0:T(8,128)S(1)} %get-tuple-element.71.rest_0_, f32[1536,512]{1,0:T(8,128)S(1)} %get-tuple-element.72.rest_1_, f32[1536,512]{1,0:T(8,128)S(1)} %get-tuple-element.73.rest_2_, ...), custom_call_target="tpu_custom_call" | custom-call | flops 3221225472 | bytes 10485760 | tf_op jit(solution)/shard_map/prefix/pallas_call | solution.py:282
  114.0 6.0 %prefix_last.1 = bf16[1536,512]{1,0:T(8,128)(2,1)} custom-call(bf16[1536,512]{1,0:T(8,128)(2,1)S(1)} %copy-done.3, f32[1536,512]{1,0:T(8,128)S(1)} %get-tuple-element.76.rest_0_, f32[1536,512]{1,0:T(8,128)S(1)} %get-tuple-element.77.rest_1_, f32[1536,512]{1,0:T(8,128)S(1)} %get-tuple-element.78.rest_2_, bf16[512,512]{1,0:T(8,128)(2,1)S(1)} %collective-permute-done.10.rest_3_), custom_call_target="tpu_custom_call" | custom-call | flops 3221225472 | bytes 10485760 | tf_op jit(solution)/shard_map/prefix_last/pallas_call | solution.py:282
  (81 shorter events, 14.5 us)
Async XLA Ops:
  0.0 8.4 %slice-start = ((bf16[1536,256]{1,0:T(8,128)(2,1)}), bf16[1024,256]{1,0:T(8,128)(2,1)S(1)}, s32[]{:S(2)}) async-start(bf16[1536,256]{1,0:T(8,128)(2,1)} %k_ref.1), calls=%async_computation.1 | async-start | bytes 1048576 | tf_op jit(solution)/shard_map/slice | solution.py:302
  0.0 8.4 %slice-start.1 = ((bf16[1536,256]{1,0:T(8,128)(2,1)}), bf16[1024,256]{1,0:T(8,128)(2,1)S(1)}, s32[]{:S(2)}) async-start(bf16[1536,256]{1,0:T(8,128)(2,1)} %v_ref.5), calls=%async_computation.2 | async-start | bytes 1048576 | tf_op jit(solution)/shard_map/slice | solution.py:302
  2.4 7.1 %collective-permute-start = (bf16[128,4096]{1,0:T(8,128)(2,1)}, bf16[128,4096]{1,0:T(8,128)(2,1)}, u32[]{:S(2)}, u32[]{:S(2)}) collective-permute-start(bf16[128,4096]{1,0:T(8,128)(2,1)} %dynamic-slice_bitcast_fusion), channel_id=1, source_target_pairs={{0,8},{8,0},{1,9},{9,1},{2,10},{10,2},{3,11},{11,3},{4,12},{12,4},... | collective-permute-start | bytes 3145736 | tf_op jit(solution)/shard_map/ppermute | solution.py:24
  9.6 7.0 %copy-start.23 = (f32[128]{0:T(128)S(1)}, f32[128]{0:T(128)}, u32[]{:S(2)}) copy-start(f32[128]{0:T(128)} %param.12) | copy-start | bytes 1540
  9.6 11.9 %copy-start.24 = (f32[128]{0:T(128)S(1)}, f32[128]{0:T(128)}, u32[]{:S(2)}) copy-start(f32[128]{0:T(128)} %param.11) | copy-start | bytes 1540
  9.6 11.9 %copy-start = (bf16[1536,256]{1,0:T(8,128)(2,1)S(1)}, bf16[1536,256]{1,0:T(8,128)(2,1)}, u32[]{:S(2)}) copy-start(bf16[1536,256]{1,0:T(8,128)(2,1)} %k_ref.1) | copy-start | bytes 2359300
  10.8 16.2 %collective-permute-start.1 = (bf16[64,4096]{1,0:T(8,128)(2,1)}, bf16[64,4096]{1,0:T(8,128)(2,1)}, u32[]{:S(2)}, u32[]{:S(2)}) collective-permute-start(bf16[64,4096]{1,0:T(8,128)(2,1)} %dynamic-slice_bitcast_fusion.1), channel_id=1, source_target_pairs={{0,128},{128,0},{1,129},{129,1},{2,130},{130,2},{3,131},{131,3},{4... | collective-permute-start | bytes 1572872 | tf_op jit(solution)/shard_map/ppermute | solution.py:24
  16.6 17.0 %collective-permute-start.2 = (bf16[1024,512]{1,0:T(8,128)(2,1)}, bf16[1024,512]{1,0:T(8,128)(2,1)S(1)}, u32[]{:S(2)}, u32[]{:S(2)}) collective-permute-start(bf16[1024,512]{1,0:T(8,128)(2,1)} %pad_maximum_fusion), channel_id=1, source_target_pairs={{0,8},{8,16},{16,24},{24,32},{32,40},{40,48},{48,56},{56,64},{64,7... | collective-permute-start | bytes 3145736 | tf_op jit(solution)/shard_map/ppermute | solution.py:304
  26.9 6.7 %copy-start.11 = (bf16[1536,256]{1,0:T(8,128)(2,1)}, bf16[1536,256]{1,0:T(8,128)(2,1)S(1)}, u32[]{:S(2)}) copy-start(bf16[1536,256]{1,0:T(8,128)(2,1)S(1)} %get-tuple-element.47.k_ref) | copy-start | bytes 2359300
  34.6 24.3 %all-to-all-start = ((bf16[64,8,512]{2,1,0:T(8,128)(2,1)}), bf16[64,8,512]{2,1,0:T(8,128)(2,1)}, u32[]{:S(2)}, u32[]{:S(2)}) async-start(bf16[64,8,512]{2,1,0:T(8,128)(2,1)} %bitcast.12), calls=%async_computation | async-start | bytes 1048576 | tf_op jit(solution)/shard_map/all_to_all | solution.py:325
  49.1 12.2 %copy-start.3 = (bf16[1536,512]{1,0:T(8,128)(2,1)S(1)}, bf16[1536,512]{1,0:T(8,128)(2,1)}, u32[]{:S(2)}) copy-start(bf16[1536,512]{1,0:T(8,128)(2,1)} %copy-done.1) | copy-start | bytes 4718596
  49.1 12.2 %copy-start.7 = (bf16[1024,512]{1,0:T(8,128)(2,1)S(1)}, bf16[1024,512]{1,0:T(8,128)(2,1)}, u32[]{:S(2)}) copy-start(bf16[1024,512]{1,0:T(8,128)(2,1)} %copy-done.5) | copy-start | bytes 3145732
  59.7 7.6 %collective-permute-start.3 = (bf16[64,512]{1,0:T(8,128)(2,1)S(1)}, bf16[64,512]{1,0:T(8,128)(2,1)S(1)}, u32[]{:S(2)}, u32[]{:S(2)}) collective-permute-start(bf16[64,512]{1,0:T(8,128)(2,1)S(1)} %dynamic-slice_bitcast_fusion.2), channel_id=1, source_target_pairs={{0,128},{128,0},{1,129},{129,1},{2,130},{130,2},{3,131},{131,3},{4... | collective-permute-start | bytes 196616 | tf_op jit(solution)/shard_map/ppermute | solution.py:24
  63.5 24.7 %copy-start.10 = (bf16[1536,256]{1,0:T(8,128)(2,1)S(1)}, bf16[1536,256]{1,0:T(8,128)(2,1)}, u32[]{:S(2)}) copy-start(bf16[1536,256]{1,0:T(8,128)(2,1)} %v_ref.5) | copy-start | bytes 2359300
  67.3 33.2 %copy-start.15 = (f32[512,512]{1,0:T(8,128)S(1)}, f32[512,512]{1,0:T(8,128)}, u32[]{:S(2)}) copy-start(f32[512,512]{1,0:T(8,128)} %copy-done.14) | copy-start | bytes 3145732
  67.3 33.2 %copy-start.17 = (f32[512,512]{1,0:T(8,128)S(1)}, f32[512,512]{1,0:T(8,128)}, u32[]{:S(2)}) copy-start(f32[512,512]{1,0:T(8,128)} %copy-done.16) | copy-start | bytes 3145732
  67.3 33.2 %copy-start.19 = (f32[512,512]{1,0:T(8,128)S(1)}, f32[512,512]{1,0:T(8,128)}, u32[]{:S(2)}) copy-start(f32[512,512]{1,0:T(8,128)} %copy-done.18) | copy-start | bytes 3145732
  67.3 24.4 %collective-permute-start.4 = (bf16[128,512]{1,0:T(8,128)(2,1)S(1)}, bf16[128,512]{1,0:T(8,128)(2,1)S(1)}, u32[]{:S(2)}, u32[]{:S(2)}) collective-permute-start(bf16[128,512]{1,0:T(8,128)(2,1)S(1)} %pad_maximum_fusion.1), channel_id=1, source_target_pairs={{0,64},{16,80},{32,96},{48,112},{64,0},{80,16},{96,32},{112,48},{1... | collective-permute-start | bytes 393224 | tf_op jit(solution)/shard_map/ppermute | solution.py:28
  72.8 19.0 %collective-permute-start.5 = (bf16[128,512]{1,0:T(8,128)(2,1)S(1)}, bf16[128,512]{1,0:T(8,128)(2,1)S(1)}, u32[]{:S(2)}, u32[]{:S(2)}) collective-permute-start(bf16[128,512]{1,0:T(8,128)(2,1)S(1)} %pad_maximum_fusion.1), channel_id=1, source_target_pairs={{0,32},{16,48},{32,64},{48,80},{64,96},{80,112},{96,0},{112,16},{1... | collective-permute-start | bytes 393224 | tf_op jit(solution)/shard_map/ppermute | solution.py:28
  73.5 18.4 %collective-permute-start.6 = (bf16[128,512]{1,0:T(8,128)(2,1)S(1)}, bf16[128,512]{1,0:T(8,128)(2,1)S(1)}, u32[]{:S(2)}, u32[]{:S(2)}) collective-permute-start(bf16[128,512]{1,0:T(8,128)(2,1)S(1)} %pad_maximum_fusion.1), channel_id=1, source_target_pairs={{0,96},{16,112},{32,0},{48,16},{64,32},{80,48},{96,64},{112,80},{1... | collective-permute-start | bytes 393224 | tf_op jit(solution)/shard_map/ppermute | solution.py:28
  91.9 8.7 %collective-permute-start.9 = (bf16[512,512]{1,0:T(8,128)(2,1)S(1)}, bf16[512,512]{1,0:T(8,128)(2,1)S(1)}, u32[]{:S(2)}, u32[]{:S(2)}) collective-permute-start(bf16[512,512]{1,0:T(8,128)(2,1)S(1)} %constant_dynamic-update-slice_fusion.2.rest_9_), channel_id=1, source_target_pairs={{0,8},{8,0},{1,9},{9,1},{2,10},{10,2},{3,11},{11,3},{4,12},{12,4},... | collective-permute-start | bytes 1572872 | tf_op jit(solution)/shard_map/ppermute | solution.py:24
  97.9 10.6 %collective-permute-start.7 = (bf16[256,512]{1,0:T(8,128)(2,1)S(1)}, bf16[256,512]{1,0:T(8,128)(2,1)S(1)}, u32[]{:S(2)}, u32[]{:S(2)}) collective-permute-start(bf16[256,512]{1,0:T(8,128)(2,1)S(1)} %get-tuple-element.80), channel_id=1, source_target_pairs={{0,16},{16,32},{32,48},{48,64},{64,80},{80,96},{96,112},{112,0},{1... | collective-permute-start | bytes 786440 | tf_op jit(solution)/shard_map/ppermute | solution.py:28
  97.9 10.6 %collective-permute-start.8 = (bf16[256,512]{1,0:T(8,128)(2,1)S(1)}, bf16[256,512]{1,0:T(8,128)(2,1)S(1)}, u32[]{:S(2)}, u32[]{:S(2)}) collective-permute-start(bf16[256,512]{1,0:T(8,128)(2,1)S(1)} %get-tuple-element.80), channel_id=1, source_target_pairs={{0,112},{16,0},{32,16},{48,32},{64,48},{80,64},{96,80},{112,96},{1... | collective-permute-start | bytes 786440 | tf_op jit(solution)/shard_map/ppermute | solution.py:28
  108.5 5.5 %collective-permute-start.10 = (bf16[512,512]{1,0:T(8,128)(2,1)S(1)}, bf16[512,512]{1,0:T(8,128)(2,1)S(1)}, u32[]{:S(2)}, u32[]{:S(2)}) collective-permute-start(bf16[512,512]{1,0:T(8,128)(2,1)S(1)} %constant_dynamic-update-slice_fusion.6.rest_3_), channel_id=1, source_target_pairs={{0,8},{8,0},{1,9},{9,1},{2,10},{10,2},{3,11},{11,3},{4,12},{12,4},... | collective-permute-start | bytes 1572872 | tf_op jit(solution)/shard_map/ppermute | solution.py:24
  (15 other events, 23.1 us)
where the time goes:
time: 121 us; the launch traced here: 120 us
  starting transfers between devices  52.6 us (43%)
  Pallas kernels  33.5 us (28%)
  local copies, waits for them, and re-layouts  16.7 us (14%)
  other arithmetic  8.63 us (7%)
  waiting for transfers between devices  7.34 us (6%)
  between operations  1.33 us (1%)
    ppermute x5, starting transfers between devices, round_z(): return lax.ppermute(array, 'z', [(i, (i + r) % NZ) for i in range(NZ)])  23.6 us
    pallas_call x3, Pallas kernels, prefix_part(): pl.pallas_call(functools.partial(prefix_kernel, last, len(states), len(pi...  18.6 us
    ppermute x5, starting transfers between devices, swapped(): return lax.ppermute(array, axis, [(0, 1), (1, 0)])  12.7 us
    all_to_all x1, starting transfers between devices, on_device(): lax.all_to_all(parts, ('z', 'head'), split_axis=0, concat_axis=0, tiled=T...  11.4 us
    unnamed x54, local copies, waits for them, and re-layouts  11.2 us
    pallas_call x3, Pallas kernels, band_part(): pl.pallas_call(functools.partial(band_kernel, part, halo_rows), grid=(1,)...  11.2 us
    ppermute x1, starting transfers between devices, on_device(): before = lax.ppermute(tail, SEQ, onward)  4.94 us
    sin x1, other arithmetic, on_device(): cosine, sine = (jnp.cos(angle), jnp.sin(angle))  4.58 us
  transfers between devices with their start and end apart: 12, of which 2 were waited for; matrix products, arithmetic and copies ran while one was open for 8% of the time, Pallas kernels for 23%

commit v1 on v0

--- a/solution.py
+++ b/solution.py
@@ -32,11 +32,72 @@
     return lax.dynamic_index_in_dim(array, at, 0, keepdims=False)
 
 
-def halved(part, axis, root_at):
-    at = lax.axis_index(axis)
-    part = part.reshape(2, part.shape[0] // 2, part.shape[1])
-    came = swapped(pick(part, 1 - at), axis)
-    return jnp.where(root_at == at, pick(part, at), came)
+def owner_at(owner_ref):
+    root = owner_ref[0]
+    return root // (NZ * NC), (root // NC) % NZ, root % NC
+
+
+def copied(source, target, sems):
+    rows = target.shape[0] // sems.shape[0]
+    copies = [
+        pltpu.make_async_copy(
+            source.at[pl.ds(i * rows, rows)], target.at[pl.ds(i * rows, rows)], sems.at[i]
+        )
+        for i in range(sems.shape[0])
+    ]
+    for copy in copies:
+        copy.start()
+    for copy in copies:
+        copy.wait()
+
+
+def other_half_kernel(slab_ref, out_ref, sems):
+    rows = out_ref.shape[0]
+    copied(slab_ref.at[pl.ds((1 - lax.axis_index("core")) * rows, rows)], out_ref, sems)
+
+
+def quarter_of(owner_ref, slab_ref, sibling_ref, of_y, out_ref, sems):
+    core, rows = lax.axis_index("core"), out_ref.shape[0]
+    mine = owner_at(owner_ref)[2] == core
+
+    @pl.when(mine)
+    def _():
+        copied(slab_ref.at[pl.ds((core * YH + of_y) * rows, rows)], out_ref, sems)
+
+    @pl.when(jnp.logical_not(mine))
+    def _():
+        copied(sibling_ref.at[pl.ds(of_y * rows, rows)], out_ref, sems)
+
+
+def far_quarter_kernel(owner_ref, slab_ref, sibling_ref, out_ref, sems):
+    quarter_of(owner_ref, slab_ref, sibling_ref, 1 - lax.axis_index("yh"), out_ref, sems)
+
+
+def own_quarter_kernel(owner_ref, slab_ref, sibling_ref, came_ref, out_ref, sems):
+    y = lax.axis_index("yh")
+    mine = owner_at(owner_ref)[0] == y
+
+    @pl.when(mine)
+    def _():
+        quarter_of(owner_ref, slab_ref, sibling_ref, y, out_ref, sems)
+
+    @pl.when(jnp.logical_not(mine))
+    def _():
+        copied(came_ref, out_ref, sems)
+
+
+def moved(kernel, rows, *operands):
+    specs = [
+        pl.BlockSpec(memory_space=pltpu.SMEM if o.dtype == jnp.int32 else pl.ANY) for o in operands
+    ]
+    return pl.pallas_call(
+        kernel,
+        out_shape=jax.ShapeDtypeStruct((rows, operands[-1].shape[1]), jnp.bfloat16),
+        in_specs=specs,
+        out_specs=pl.BlockSpec(memory_space=pl.ANY),
+        scratch_shapes=[pltpu.SemaphoreType.DMA((4,))],
+        name="slab_rows",
+    )(*operands)
 
 
 def tables(cos_ref, sin_ref, at, gain, scale):
@@ -74,19 +135,43 @@
     return jnp.concatenate([ref[at, columns_of(h)] for h in heads], axis=0)
 
 
-def prep_kernel(q_ref, k_ref, qg_ref, kg_ref, cos_ref, sin_ref, qn_ref, kn_ref):
+def prep_kernel(
+    q_ref, k_ref, qg_ref, kg_ref, cos_ref, sin_ref, qn_ref, kn_ref, qi_ref, ki_ref, qs_ref, ks_ref, in_sems, out_sems
+):
+    tiles = q_ref.shape[0] // BAND_TILE
+
+    def copies(t, pairs, sems):
+        at = rows_at(t, BAND_TILE)
+        return [
+            pltpu.make_async_copy(source.at[at], target.at[at], sems.at[i, t])
+            for i, (source, target) in enumerate(pairs)
+        ]
+
+    into = ((q_ref, qi_ref), (k_ref, ki_ref))
+    out = ((qs_ref, qn_ref), (ks_ref, kn_ref))
+    for t in range(tiles):
+        for copy in copies(t, into, in_sems):
+            copy.start()
+
     def own(t, _):
         at = rows_at(t, BAND_TILE)
         at_table = rows_at(t + WINDOW // BAND_TILE, BAND_TILE)
         q_tables = tables(cos_ref, sin_ref, at_table, qg_ref[...], QSCALAR ** (-0.5))
         k_tables = tables(cos_ref, sin_ref, at_table, kg_ref[...], 1.0)
+        for copy in copies(t, into, in_sems):
+            copy.wait()
         for c in range(k_ref.shape[1] // HD):
-            kn_ref[at, columns_of(c)] = normed(k_ref[at, columns_of(c)], *k_tables)
+            ks_ref[at, columns_of(c)] = normed(ki_ref[at, columns_of(c)], *k_tables)
         for h in range(q_ref.shape[1] // HD):
-            qn_ref[at, columns_of(h)] = normed(q_ref[at, columns_of(h)], *q_tables)
+            qs_ref[at, columns_of(h)] = normed(qi_ref[at, columns_of(h)], *q_tables)
+        for copy in copies(t, out, out_sems):
+            copy.start()
         return 0
 
-    lax.fori_loop(0, q_ref.shape[0] // BAND_TILE, own, 0)
+    lax.fori_loop(0, tiles, own, 0)
+    for t in range(tiles):
+        for copy in copies(t, out, out_sems):
+            copy.wait()
 
 
 def halo_kernel(k_ref, kg_ref, cos_ref, sin_ref, kn_ref):
@@ -124,10 +209,31 @@
     return top, summed, total
 
 
-def band_kernel(part, halo_rows, first_ref, q_ref, k_ref, v_ref, *rest):
-    kb_ref, vb_ref = rest[:2] if halo_rows else (None, None)
-    outs = rest[-3:]
-    kv = k_ref.shape[1] // HD
+def band_kernel(part, halo_rows, to_hbm, first_ref, *rest):
+    count = 5 if halo_rows else 3
+    sources, outs, rest = rest[:count], rest[count : count + 3], rest[count + 3 :]
+    held, in_sems, rest = rest[:count], rest[count], rest[count + 1 :]
+    rows, kv = held[0].shape[0], held[1].shape[1] // HD
+    before_at = pl.ds(WINDOW - halo_rows, halo_rows)
+    whats = [
+        sources[0].at[pl.ds(part * rows, rows)],
+        sources[1].at[pl.ds(0, (part + 1) * rows)],
+        sources[2].at[pl.ds(0, (part + 1) * rows)],
+    ]
+    if halo_rows:
+        whats += [sources[3].at[before_at], sources[4].at[before_at, pl.ds(kv * HD, kv * HD)]]
+    copies = [
+        pltpu.make_async_copy(what, where, in_sems.at[i])
+        for i, (what, where) in enumerate(zip(whats, held))
+    ]
+    for copy in copies:
+        copy.start()
+    for copy in copies:
+        copy.wait()
+    q_ref, k_ref, v_ref = held[:3]
+    kb_ref, vb_ref = held[3:] if halo_rows else (None, None)
+    stores, out_sems = (rest[:3], rest[3]) if to_hbm else (outs, None)
+
     group = q_ref.shape[1] // HD // kv
     rows_in = lax.broadcasted_iota(jnp.int32, (group * BAND_TILE, CHUNK), 0) % BAND_TILE
     columns_in = lax.broadcasted_iota(jnp.int32, (group * BAND_TILE, CHUNK), 1)
@@ -135,7 +241,8 @@
     late = columns_in <= rows_in
     reach = WINDOW // CHUNK
     is_first = first_ref[0] == 1
-    tiles = q_ref.shape[0] // BAND_TILE
+    tiles = rows // BAND_TILE
+    sent = []
     for t in range(tiles):
         at = slice(t * BAND_TILE, (t + 1) * BAND_TILE)
         queries = [stacked(q_ref, at, range(c * group, (c + 1) * group)) for c in range(kv)]
@@ -156,9 +263,17 @@
                 )
         for c in range(kv):
             for g in range(group):
-                rows = slice(g * BAND_TILE, (g + 1) * BAND_TILE)
-                for ref, value in zip(outs, state[c]):
-                    ref[at, columns_of(c * group + g)] = value[rows]
+                of_head = slice(g * BAND_TILE, (g + 1) * BAND_TILE)
+                for ref, value in zip(stores, state[c]):
+                    ref[at, columns_of(c * group + g)] = value[of_head]
+        if to_hbm:
+            at_rows = pl.ds(t * BAND_TILE, BAND_TILE)
+            for i in range(3):
+                copy = pltpu.make_async_copy(stores[i].at[at_rows], outs[i].at[at_rows], out_sems.at[i, t])
+                copy.start()
+                sent.append(copy)
+    for copy in sent:
+        copy.wait()
 
 
 def blocks_of(p_refs):
@@ -187,6 +302,13 @@
 def prefix_kernel(last, bands, pieces, q_ref, *rest):
     states, rest = [rest[3 * i : 3 * i + 3] for i in range(bands)], rest[3 * bands :]
     p_refs, outs = rest[:pieces], rest[pieces:]
+    if last:
+        out_ref, store_ref, sems = outs
+        outs = (store_ref,)
+        sent = [
+            pltpu.make_async_copy(store_ref.at[rows_at(t, TILE)], out_ref.at[rows_at(t, TILE)], sems.at[t])
+            for t in range(q_ref.shape[0] // TILE)
+        ]
     kv = p_refs[0].shape[1] // (2 * HD)
     group = q_ref.shape[1] // HD // kv
     each = states[0][0].shape[0]
@@ -209,6 +331,12 @@
     if bands > 1:
         for i in range(q_ref.shape[0] // TILE):
             step(i, states[i * TILE // each], slice(i * TILE % each, i * TILE % each + TILE))
+    elif last:
+        for t in range(q_ref.shape[0] // TILE):
+            step(t, states[0], slice(t * TILE, (t + 1) * TILE))
+            sent[t].start()
+        for copy in sent:
+            copy.wait()
     else:
 
         def one(t, _):
@@ -219,6 +347,8 @@
 
 
 WHOLE = pl.BlockSpec(memory_space=pltpu.VMEM)
+ALONE = pltpu.CompilerParams(vmem_limit_bytes=60 * 1024 * 1024)
+IN_HBM = pl.BlockSpec(memory_space=pltpu.HBM)
 PARAMS = pltpu.CompilerParams(vmem_limit_bytes=VMEM_LIMIT)
 
 
@@ -226,56 +356,66 @@
     return pl.CostEstimate(flops=8 * pairs * HD, transcendentals=pairs, bytes_accessed=in_out)
 
 
-def normed_part(kernel, outs, *args):
-    size = sum(o.size for o in outs)
+def prep(*args):
+    q, k = args[:2]
+    tiles = q.shape[0] // BAND_TILE
     return pl.pallas_call(
-        kernel,
-        out_shape=outs,
-        in_specs=[WHOLE] * len(args),
-        out_specs=(WHOLE,) * len(outs),
-        compiler_params=PARAMS,
-        cost_estimate=pl.CostEstimate(flops=60 * size, transcendentals=size // HD, bytes_accessed=6 * size),
+        prep_kernel,
+        out_shape=tuple(jax.ShapeDtypeStruct(a.shape, jnp.bfloat16) for a in (q, k)),
+        in_specs=[IN_HBM] * 2 + [WHOLE] * 4,
+        out_specs=(IN_HBM,) * 2,
+        scratch_shapes=[pltpu.VMEM(a.shape, jnp.bfloat16) for a in (q, k, q, k)]
+        + [pltpu.SemaphoreType.DMA((2, tiles))] * 2,
+        compiler_params=ALONE,
+        cost_estimate=pl.CostEstimate(flops=q.size, transcendentals=0, bytes_accessed=q.size),
         name="norm_rope",
     )(*args)
+
+
+def halo_keys(before, *args):
+    return pl.pallas_call(
+        halo_kernel,
+        out_shape=jax.ShapeDtypeStruct((WINDOW, before.shape[1] // 2), jnp.bfloat16),
+        in_specs=[WHOLE] * 4,
+        out_specs=WHOLE,
+        compiler_params=PARAMS,
+        cost_estimate=pl.CostEstimate(flops=30 * before.size, transcendentals=0, bytes_accessed=4 * before.size),
+        name="norm_rope_halo",
+    )(before, *args)
 
 
 def band_part(part, parts, first, q, k, v, key_before, before):
     width, wide = q.shape[1], k.shape[1]
     rows = q.shape[0] // parts
     halo_rows = max(0, WINDOW - part * rows)
-    own = pl.BlockSpec(((part + 1) * rows, wide), lambda i: (0, 0))
-    operands = [first, q, k, v]
-    in_specs = [
-        pl.BlockSpec(memory_space=pltpu.SMEM),
-        pl.BlockSpec((rows, width), lambda i: (part, 0)),
-        own,
-        own,
-    ]
-    if halo_rows:
-        at = WINDOW // halo_rows - 1
-        operands += [key_before, before]
-        in_specs += [
-            pl.BlockSpec((halo_rows, wide), lambda i: (at, 0)),
-            pl.BlockSpec((halo_rows, wide), lambda i: (at, 1)),
-        ]
+    operands = [q, k, v] + ([key_before, before] if halo_rows else [])
+    shapes = [(rows, width)] + [((part + 1) * rows, wide)] * 2 + ([(halo_rows, wide)] * 2 if halo_rows else [])
+    scratch = [pltpu.VMEM(shape, jnp.bfloat16) for shape in shapes]
+    scratch.append(pltpu.SemaphoreType.DMA((len(shapes),)))
+    to_hbm = part < parts - 1
+    if to_hbm:
+        scratch += [pltpu.VMEM((rows, width), jnp.float32)] * 3
+        scratch.append(pltpu.SemaphoreType.DMA((3, rows // BAND_TILE)))
     return pl.pallas_call(
-        functools.partial(band_kernel, part, halo_rows),
-        grid=(1,),
+        functools.partial(band_kernel, part, halo_rows, to_hbm),
         out_shape=(jax.ShapeDtypeStruct((rows, width), jnp.float32),) * 3,
-        in_specs=in_specs,
-        out_specs=(WHOLE,) * 3,
-        compiler_params=PARAMS,
+        in_specs=[pl.BlockSpec(memory_space=pltpu.SMEM)] + [IN_HBM] * len(operands),
+        out_specs=(IN_HBM if to_hbm else WHOLE,) * 3,
+        scratch_shapes=scratch,
+        compiler_params=ALONE if to_hbm else PARAMS,
         cost_estimate=cost(rows * (width // HD) * (WINDOW + BAND_TILE), 5 << 20),
         name="band",
-    )(*operands)
+    )(first, *operands)
 
 
 def prefix_part(last, q, states, *pieces):
     local, width = q.shape
     flat = [part for state in states for part in state]
+    scratch = []
     if last:
         out_shape = jax.ShapeDtypeStruct((local, width), jnp.bfloat16)
-        out_specs = WHOLE
+        out_specs = IN_HBM
+        scratch = [pltpu.VMEM((local, width), jnp.bfloat16), pltpu.SemaphoreType.DMA((local // TILE,))]
     else:
         out_shape = (jax.ShapeDtypeStruct((local, width), jnp.float32),) * 3
         out_specs = (WHOLE,) * 3
@@ -284,6 +424,7 @@
         out_shape=out_shape,
         in_specs=[WHOLE] * (1 + len(flat) + len(pieces)),
         out_specs=out_specs,
+        scratch_shapes=scratch,
         compiler_params=PARAMS,
         cost_estimate=cost(local * (width // HD) * sum(p.shape[0] for p in pieces), 10 << 20),
         name="prefix_last" if last else "prefix",
@@ -293,41 +434,34 @@
 def on_device(queries, keys, values, q_gain, k_gain, positions, prefix_cache, owner):
     local = queries.shape[0]
     root = owner[0]
-    root_y, root_z, root_c = root // (NZ * NC), (root // NC) % NZ, root % NC
+    root_z = (root // NC) % NZ
     q_gain, k_gain = (1.0 + q_gain)[None], (1.0 + k_gain)[None]
     first = (lax.axis_index(SEQ) == 0).astype(jnp.int32).reshape(1)
 
-    slab = halved(prefix_cache[0], "core", root_c)
+    whole = prefix_cache[0]
+    half_rows = whole.shape[0] // NC
+    sibling = swapped(moved(other_half_kernel, half_rows, whole), "core")
     onward = [(i, i + 1) for i in range(YH * NZ * NC - 1)]
     tail = jnp.concatenate([keys[local - WINDOW :], values[local - WINDOW :]], axis=1)
-    slab, tail = lax.optimization_barrier((slab, tail))
+    sent = moved(far_quarter_kernel, half_rows // YH, owner, whole, sibling)
+    sent, tail = lax.optimization_barrier((sent, tail))
     before = lax.ppermute(tail, SEQ, onward)
-    slab = halved(slab, "yh", root_y)
+    came = swapped(sent, "yh")
+    slab = moved(own_quarter_kernel, half_rows // YH, owner, whole, sibling, came)
 
     half = HD // 2
     freq = 10000.0 ** (-(jnp.arange(half).astype(jnp.float32) * 2.0) / HD)
     extended = positions[0] + jnp.arange(-WINDOW, local, dtype=jnp.int32)
     angle = extended.astype(jnp.float32)[:, None] * freq[None, :]
     cosine, sine = jnp.cos(angle), jnp.sin(angle)
-    query, key = normed_part(
-        prep_kernel,
-        (
-            jax.ShapeDtypeStruct(queries.shape, jnp.bfloat16),
-            jax.ShapeDtypeStruct(keys.shape, jnp.bfloat16),
-        ),
-        queries, keys, q_gain, k_gain, cosine, sine,
-    )
+    query, key = prep(queries, keys, q_gain, k_gain, cosine, sine)
     slab, query, before = lax.optimization_barrier((slab, query, before))
 
     rows, wide = slab.shape
     parts = slab.reshape(NZ, rows // NZ, NH, wide // NH).transpose(0, 2, 1, 3)
     parts = parts.reshape(NZ * NH, rows // NZ, wide // NH)
     parts = lax.all_to_all(parts, ("z", "head"), split_axis=0, concat_axis=0, tiled=True)
-    (key_before,) = normed_part(
-        halo_kernel,
-        (jax.ShapeDtypeStruct((WINDOW, keys.shape[1]), jnp.bfloat16),),
-        before, k_gain, cosine, sine,
-    )
+    key_before = halo_keys(before, k_gain, cosine, sine)
 
     def band(part, first):
         return band_part(part, 3, first, query, key, values, key_before, before)

time: 121 us -> 177 us (1.46)
  Pallas kernels: 33.5 us -> 110 us
  starting transfers between devices: 52.6 us -> 28.5 us
  waiting for transfers between devices: 7.34 us -> 24 us
  local copies, waits for them, and re-layouts: 16.7 us -> 3.98 us
    pallas_call x5 -> x8, Pallas kernels: 15 us -> 92.2 us  [the longest x3 66.9 us: moved(): pl.pallas_call(kernel, out_shape=jax.ShapeDtypeStruct((rows, operands[-1]...]
    ppermute x5, starting transfers between devices: 23.6 us -> 9.73 us  [round_z(): return lax.ppermute(array, 'z', [(i, (i + r) % NZ) for i in range(NZ)])]
    ppermute x5, waiting for transfers between devices: 0.01 us -> 9.74 us  [swapped(): return lax.ppermute(array, axis, [(0, 1), (1, 0)])]
    unnamed x54 -> x38, local copies, waits for them, and re-layouts: 11.2 us -> 2.73 us
    ppermute x5, waiting for transfers between devices: 0.01 us -> 6.96 us  [round_z(): return lax.ppermute(array, 'z', [(i, (i + r) % NZ) for i in range(NZ)])]
    all_to_all x1, starting transfers between devices: 11.4 us -> 5.16 us  [on_device(): lax.all_to_all(parts, ('z', 'head'), split_axis=0, concat_axis=0, tiled=T...]
    ppermute x1, waiting for transfers between devices: 4.44 us -> 0.01 us  [on_device(): before = lax.ppermute(tail, SEQ, onward)]
    all_to_all x1, waiting for transfers between devices: 2.87 us -> 7.27 us  [on_device(): lax.all_to_all(parts, ('z', 'head'), split_axis=0, concat_axis=0, tiled=T...]
  transfers between devices with their start and end apart: 12 -> 12, of which waited for: 2 -> 4; matrix products, arithmetic and copies ran while one was open for 8% -> 6% of each run, Pallas kernels for 23% -> 31%
where the time goes in v1:
time: 177 us
  Pallas kernels  110 us (62%)
  starting transfers between devices  28.5 us (16%)
  waiting for transfers between devices  24 us (14%)
  other arithmetic  8.98 us (5%)
  local copies, waits for them, and re-layouts  3.98 us (2%)
    pallas_call x3, Pallas kernels, moved(): pl.pallas_call(kernel, out_shape=jax.ShapeDtypeStruct((rows, operands[-1]...  66.9 us
    pallas_call x3, Pallas kernels, prefix_part(): pl.pallas_call(functools.partial(prefix_kernel, last, len(states), len(pi...  17.7 us
    pallas_call x3, Pallas kernels, band_part(): pl.pallas_call(functools.partial(band_kernel, part, halo_rows, to_hbm), o...  16.4 us
    ppermute x5, starting transfers between devices, swapped(): return lax.ppermute(array, axis, [(0, 1), (1, 0)])  11.7 us
    ppermute x5, waiting for transfers between devices, swapped(): return lax.ppermute(array, axis, [(0, 1), (1, 0)])  9.74 us
    ppermute x5, starting transfers between devices, round_z(): return lax.ppermute(array, 'z', [(i, (i + r) % NZ) for i in range(NZ)])  9.73 us
    all_to_all x1, waiting for transfers between devices, on_device(): lax.all_to_all(parts, ('z', 'head'), split_axis=0, concat_axis=0, tiled=T...  7.27 us
    ppermute x5, waiting for transfers between devices, round_z(): return lax.ppermute(array, 'z', [(i, (i + r) % NZ) for i in range(NZ)])  6.96 us
  transfers between devices with their start and end apart: 12, of which 4 were waited for; matrix products, arithmetic and copies ran while one was open for 6% of the time, Pallas kernels for 31%

profile of v1, /device:TPU:1, one launch (start us, length us, event | category | flops | bytes accessed | tf_op | source)
XLA Modules:
  0.0 176.7 jit_solution(3059296321589613179)
XLA Ops:
  0.0 32.9 %slab_rows.3 = bf16[128,4096]{1,0:T(8,128)(2,1)} custom-call(bf16[256,4096]{1,0:T(8,128)(2,1)} %bitcast.20), custom_call_target="tpu_custom_call" | custom-call | tf_op jit(solution)/shard_map/slab_rows/pallas_call | solution.py:93
  32.9 3.3 %collective-permute-start = (bf16[128,4096]{1,0:T(8,128)(2,1)}, bf16[128,4096]{1,0:T(8,128)(2,1)S(1)}, u32[]{:S(2)}, u32[]{:S(2)}) collective-permute-start(bf16[128,4096]{1,0:T(8,128)(2,1)} %slab_rows.3), channel_id=1, source_target_pairs={{0,8},{8,0},{1,9},{9,1},{2,10},{10,2},{3,11},{11,3},{4,12},{12,4},... | collective-permute-start | bytes 3145736 | tf_op jit(solution)/shard_map/ppermute | solution.py:24
  41.3 17.0 %slab_rows.4 = bf16[64,4096]{1,0:T(8,128)(2,1)} custom-call(s32[1]{0:T(128)} %copy.14.owner_ref, bf16[256,4096]{1,0:T(8,128)(2,1)} %bitcast.21, bf16[128,4096]{1,0:T(8,128)(2,1)} %copy-done.13), custom_call_target="tpu_custom_call" | custom-call | tf_op jit(solution)/shard_map/slab_rows/pallas_call | solution.py:93
  58.3 1.9 %collective-permute-start.2 = (bf16[1024,512]{1,0:T(8,128)(2,1)}, bf16[1024,512]{1,0:T(8,128)(2,1)}, u32[]{:S(2)}, u32[]{:S(2)}) collective-permute-start(bf16[1024,512]{1,0:T(8,128)(2,1)} %pad_maximum_fusion), channel_id=1, source_target_pairs={{0,8},{8,16},{16,24},{24,32},{32,40},{40,48},{48,56},{56,64},{64,7... | collective-permute-start | bytes 3145736 | tf_op jit(solution)/shard_map/ppermute | solution.py:448
  60.9 2.7 %collective-permute-start.1 = (bf16[64,4096]{1,0:T(8,128)(2,1)}, bf16[64,4096]{1,0:T(8,128)(2,1)S(1)}, u32[]{:S(2)}, u32[]{:S(2)}) collective-permute-start(bf16[64,4096]{1,0:T(8,128)(2,1)} %slab_rows.4), channel_id=1, source_target_pairs={{0,128},{128,0},{1,129},{129,1},{2,130},{130,2},{3,131},{131,3},{4... | collective-permute-start | bytes 1572872 | tf_op jit(solution)/shard_map/ppermute | solution.py:24
  63.6 6.2 %multiply_sine_fusion = (f32[2560,64]{1,0:T(8,128)}, f32[2560,64]{1,0:T(8,128)}) fusion(f32[64]{0:T(128)S(1)} %multiply_power_fusion, f32[2560]{0:T(1024)S(1)} %add_convert_fusion), kind=kLoop, calls=%fused_computation | loop fusion | flops 163840 | bytes 1321216 | tf_op jit(solution)/shard_map/sin | solution.py:456
  69.8 6.7 %norm_rope.1 = (bf16[1536,512]{1,0:T(8,128)(2,1)}, bf16[1536,256]{1,0:T(8,128)(2,1)}) custom-call(bf16[1536,512]{1,0:T(8,128)(2,1)} %q_ref.1, bf16[1536,256]{1,0:T(8,128)(2,1)} %k_ref.1, f32[1,128]{1,0:T(1,128)} %add_bitcast_fusion.1.qg_ref, f32[1,128]{1,0:T(1,128)} %add_bitcast_fusion.kg_ref, f32[2560,64]{1,0:T(8,128)} %get-tuple-element.84.cos_ref, ...), custom_call_target="tpu_custom_call" | custom-call | flops 786432 | bytes 786432 | tf_op jit(solution)/shard_map/norm_rope/pallas_call | solution.py:362
  76.6 9.7 %collective-permute-done.1.came_ref = bf16[64,4096]{1,0:T(8,128)(2,1)S(1)} collective-permute-done((bf16[64,4096]{1,0:T(8,128)(2,1)}, bf16[64,4096]{1,0:T(8,128)(2,1)S(1)}, u32[]{:S(2)}, u32[]{:S(2)}) %collective-permute-start.1) | collective-permute-done | bytes 524320 | tf_op jit(solution)/shard_map/ppermute | solution.py:24
  87.1 17.0 %slab_rows.5 = bf16[64,4096]{1,0:T(8,128)(2,1)} custom-call(s32[1]{0:T(128)} %copy.14.owner_ref, bf16[256,4096]{1,0:T(8,128)(2,1)} %bitcast.22, bf16[128,4096]{1,0:T(8,128)(2,1)} %copy-done.13, bf16[64,4096]{1,0:T(8,128)(2,1)} %copy-done.14), custom_call_target="tpu_custom_call" | custom-call | tf_op jit(solution)/shard_map/slab_rows/pallas_call | solution.py:93
  104.1 5.2 %all-to-all-start = ((bf16[64,8,512]{2,1,0:T(8,128)(2,1)}), bf16[64,8,512]{2,1,0:T(8,128)(2,1)S(1)}, u32[]{:S(2)}, u32[]{:S(2)}) async-start(bf16[64,8,512]{2,1,0:T(8,128)(2,1)} %bitcast.23), calls=%async_computation | async-start | bytes 1048576 | tf_op jit(solution)/shard_map/all_to_all | solution.py:463
  109.4 2.2 %norm_rope_halo.1.rest_3_ = bf16[1024,256]{1,0:T(8,128)(2,1)S(1)} custom-call(bf16[1024,512]{1,0:T(8,128)(2,1)} %collective-permute-done.2.k_ref.rest_4_, f32[1,128]{1,0:T(1,128)S(1)} %copy-done.5, f32[2560,64]{1,0:T(8,128)S(1)} %copy-done.1, f32[2560,64]{1,0:T(8,128)S(1)} %copy-done), custom_call_target="tpu_custom_call" | custom-call | flops 15728640 | bytes 2097152 | tf_op jit(solution)/shard_map/norm_rope_halo/pallas_call | solution.py:376
  112.4 6.4 %band.3 = (f32[512,512]{1,0:T(8,128)}, f32[512,512]{1,0:T(8,128)}, f32[512,512]{1,0:T(8,128)}) custom-call(s32[1]{0:T(128)} %bitcast.7.first_ref, bf16[1536,512]{1,0:T(8,128)(2,1)} %get-tuple-element.45.rest_0_.q_ref, bf16[1536,256]{1,0:T(8,128)(2,1)} %get-tuple-element.47.rest_1_, bf16[1536,256]{1,0:T(8,128)(2,1)} %rest_2_.5, bf16[1024,256]{1,0:T(8,128)(2,1)} %copy-done.3, ...), custom_call_target="tpu_custom_call" | custom-call | flops 2684354560 | bytes 5242880 | tf_op jit(solution)/shard_map/band/pallas_call | solution.py:399
  118.8 7.3 %all-to-all-done = bf16[64,8,512]{2,1,0:T(8,128)(2,1)S(1)} async-done(((bf16[64,8,512]{2,1,0:T(8,128)(2,1)}), bf16[64,8,512]{2,1,0:T(8,128)(2,1)S(1)}, u32[]{:S(2)}, u32[]{:S(2)}) %all-to-all-start) | async-done | bytes 524320 | tf_op jit(solution)/shard_map/all_to_all | solution.py:463
  126.1 3.4 %collective-permute-start.3 = (bf16[64,512]{1,0:T(8,128)(2,1)S(1)}, bf16[64,512]{1,0:T(8,128)(2,1)S(1)}, u32[]{:S(2)}, u32[]{:S(2)}) collective-permute-start(bf16[64,512]{1,0:T(8,128)(2,1)S(1)} %dynamic-slice_bitcast_fusion), channel_id=1, source_target_pairs={{0,128},{128,0},{1,129},{129,1},{2,130},{130,2},{3,131},{131,3},{4... | collective-permute-start | bytes 196616 | tf_op jit(solution)/shard_map/ppermute | solution.py:24
  129.5 6.3 %band.4 = (f32[512,512]{1,0:T(8,128)}, f32[512,512]{1,0:T(8,128)}, f32[512,512]{1,0:T(8,128)}) custom-call(s32[1]{0:T(128)} %bitcast.7.first_ref, bf16[1536,512]{1,0:T(8,128)(2,1)} %get-tuple-element.45.rest_0_.q_ref, bf16[1536,256]{1,0:T(8,128)(2,1)} %get-tuple-element.47.rest_1_, bf16[1536,256]{1,0:T(8,128)(2,1)} %rest_2_.5, bf16[1024,256]{1,0:T(8,128)(2,1)} %copy-done.3, ...), custom_call_target="tpu_custom_call" | custom-call | flops 2684354560 | bytes 5242880 | tf_op jit(solution)/shard_map/band/pallas_call | solution.py:399
  135.9 3.5 %collective-permute-start.4 = (bf16[128,512]{1,0:T(8,128)(2,1)S(1)}, bf16[128,512]{1,0:T(8,128)(2,1)S(1)}, u32[]{:S(2)}, u32[]{:S(2)}) collective-permute-start(bf16[128,512]{1,0:T(8,128)(2,1)S(1)} %pad_maximum_fusion.1), channel_id=1, source_target_pairs={{0,64},{16,80},{32,96},{48,112},{64,0},{80,16},{96,32},{112,48},{1... | collective-permute-start | bytes 393224 | tf_op jit(solution)/shard_map/ppermute | solution.py:28
  139.4 2.0 %collective-permute-start.5 = (bf16[128,512]{1,0:T(8,128)(2,1)S(1)}, bf16[128,512]{1,0:T(8,128)(2,1)S(1)}, u32[]{:S(2)}, u32[]{:S(2)}) collective-permute-start(bf16[128,512]{1,0:T(8,128)(2,1)S(1)} %pad_maximum_fusion.1), channel_id=1, source_target_pairs={{0,32},{16,48},{32,64},{48,80},{64,96},{80,112},{96,0},{112,16},{1... | collective-permute-start | bytes 393224 | tf_op jit(solution)/shard_map/ppermute | solution.py:28
  143.0 3.6 %band.5 = (f32[512,512]{1,0:T(8,128)S(1)}, f32[512,512]{1,0:T(8,128)S(1)}, f32[512,512]{1,0:T(8,128)S(1)}) custom-call(s32[1]{0:T(128)} %bitcast.7.first_ref, bf16[1536,512]{1,0:T(8,128)(2,1)S(1)} %copy-done.2, bf16[1536,256]{1,0:T(8,128)(2,1)S(1)} %copy-done.6, bf16[1536,256]{1,0:T(8,128)(2,1)S(1)} %copy-done.4), custom_call_target="tpu_custom_call" | custom-call | flops 2684354560 | bytes 5242880 | tf_op jit(solution)/shard_map/band/pallas_call | solution.py:399
  146.6 3.5 %collective-permute-done.5 = bf16[128,512]{1,0:T(8,128)(2,1)S(1)} collective-permute-done((bf16[128,512]{1,0:T(8,128)(2,1)S(1)}, bf16[128,512]{1,0:T(8,128)(2,1)S(1)}, u32[]{:S(2)}, u32[]{:S(2)}) %collective-permute-start.5) | collective-permute-done | bytes 131104 | tf_op jit(solution)/shard_map/ppermute | solution.py:28
  150.1 3.4 %collective-permute-done.6 = bf16[128,512]{1,0:T(8,128)(2,1)S(1)} collective-permute-done((bf16[128,512]{1,0:T(8,128)(2,1)S(1)}, bf16[128,512]{1,0:T(8,128)(2,1)S(1)}, u32[]{:S(2)}, u32[]{:S(2)}) %collective-permute-start.6) | collective-permute-done | bytes 131104 | tf_op jit(solution)/shard_map/ppermute | solution.py:28
  156.1 1.6 collective-permute-start.8
  157.7 7.9 %prefix.2 = (f32[1536,512]{1,0:T(8,128)S(1)}, f32[1536,512]{1,0:T(8,128)S(1)}, f32[1536,512]{1,0:T(8,128)S(1)}) custom-call(bf16[1536,512]{1,0:T(8,128)(2,1)S(1)} %copy-done.2, f32[512,512]{1,0:T(8,128)S(1)} %copy-done.7, f32[512,512]{1,0:T(8,128)S(1)} %copy-done.8, f32[512,512]{1,0:T(8,128)S(1)} %copy-done.9, f32[512,512]{1,0:T(8,128)S(1)} %copy-done.10, ...), custom_call_target="tpu_custom_call" | custom-call | flops 6442450944 | bytes 10485760 | tf_op jit(solution)/shard_map/prefix/pallas_call | solution.py:422
  166.7 4.7 %prefix.3 = (f32[1536,512]{1,0:T(8,128)S(1)}, f32[1536,512]{1,0:T(8,128)S(1)}, f32[1536,512]{1,0:T(8,128)S(1)}) custom-call(bf16[1536,512]{1,0:T(8,128)(2,1)S(1)} %copy-done.2, f32[1536,512]{1,0:T(8,128)S(1)} %get-tuple-element.71.rest_0_, f32[1536,512]{1,0:T(8,128)S(1)} %get-tuple-element.72.rest_1_, f32[1536,512]{1,0:T(8,128)S(1)} %get-tuple-element.73.rest_2_, ...), custom_call_target="tpu_custom_call" | custom-call | flops 3221225472 | bytes 10485760 | tf_op jit(solution)/shard_map/prefix/pallas_call | solution.py:422
  171.4 5.1 %prefix_last.1 = bf16[1536,512]{1,0:T(8,128)(2,1)} custom-call(bf16[1536,512]{1,0:T(8,128)(2,1)S(1)} %copy-done.2, f32[1536,512]{1,0:T(8,128)S(1)} %get-tuple-element.76.rest_0_, f32[1536,512]{1,0:T(8,128)S(1)} %get-tuple-element.77.rest_1_, f32[1536,512]{1,0:T(8,128)S(1)} %get-tuple-element.78.rest_2_, bf16[512,512]{1,0:T(8,128)(2,1)S(1)} %collective-permute-done.10.rest_3_), custom_call_target="tpu_custom_call" | custom-call | flops 3221225472 | bytes 10485760 | tf_op jit(solution)/shard_map/prefix_last/pallas_call | solution.py:422
  (64 shorter events, 11.8 us)
Async XLA Ops:
  0.0 38.7 %slice-start = ((bf16[1536,256]{1,0:T(8,128)(2,1)}), bf16[1024,256]{1,0:T(8,128)(2,1)S(1)}, s32[]{:S(2)}) async-start(bf16[1536,256]{1,0:T(8,128)(2,1)} %rest_2_.5), calls=%async_computation.1 | async-start | bytes 1048576 | tf_op jit(solution)/shard_map/slice | solution.py:445
  0.0 38.7 %slice-start.1 = ((bf16[1536,256]{1,0:T(8,128)(2,1)}), bf16[1024,256]{1,0:T(8,128)(2,1)S(1)}, s32[]{:S(2)}) async-start(bf16[1536,256]{1,0:T(8,128)(2,1)} %k_ref.1), calls=%async_computation.2 | async-start | bytes 1048576 | tf_op jit(solution)/shard_map/slice | solution.py:445
  32.9 7.4 %collective-permute-start = (bf16[128,4096]{1,0:T(8,128)(2,1)}, bf16[128,4096]{1,0:T(8,128)(2,1)S(1)}, u32[]{:S(2)}, u32[]{:S(2)}) collective-permute-start(bf16[128,4096]{1,0:T(8,128)(2,1)} %slab_rows.3), channel_id=1, source_target_pairs={{0,8},{8,0},{1,9},{9,1},{2,10},{10,2},{3,11},{11,3},{4,12},{12,4},... | collective-permute-start | bytes 3145736 | tf_op jit(solution)/shard_map/ppermute | solution.py:24
  39.8 20.5 %copy-start.16 = (f32[128]{0:T(128)S(1)}, f32[128]{0:T(128)}, u32[]{:S(2)}) copy-start(f32[128]{0:T(128)} %param.11) | copy-start | bytes 1540
  58.3 45.8 %collective-permute-start.2 = (bf16[1024,512]{1,0:T(8,128)(2,1)}, bf16[1024,512]{1,0:T(8,128)(2,1)}, u32[]{:S(2)}, u32[]{:S(2)}) collective-permute-start(bf16[1024,512]{1,0:T(8,128)(2,1)} %pad_maximum_fusion), channel_id=1, source_target_pairs={{0,8},{8,16},{16,24},{24,32},{32,40},{40,48},{48,56},{56,64},{64,7... | collective-permute-start | bytes 3145736 | tf_op jit(solution)/shard_map/ppermute | solution.py:448
  60.9 25.4 %collective-permute-start.1 = (bf16[64,4096]{1,0:T(8,128)(2,1)}, bf16[64,4096]{1,0:T(8,128)(2,1)S(1)}, u32[]{:S(2)}, u32[]{:S(2)}) collective-permute-start(bf16[64,4096]{1,0:T(8,128)(2,1)} %slab_rows.4), channel_id=1, source_target_pairs={{0,128},{128,0},{1,129},{129,1},{2,130},{130,2},{3,131},{131,3},{4... | collective-permute-start | bytes 1572872 | tf_op jit(solution)/shard_map/ppermute | solution.py:24
  76.5 32.8 %copy-start = (f32[2560,64]{1,0:T(8,128)S(1)}, f32[2560,64]{1,0:T(8,128)}, u32[]{:S(2)}) copy-start(f32[2560,64]{1,0:T(8,128)} %get-tuple-element.83.sin_ref) | copy-start | bytes 1966084
  76.6 32.8 %copy-start.1 = (f32[2560,64]{1,0:T(8,128)S(1)}, f32[2560,64]{1,0:T(8,128)}, u32[]{:S(2)}) copy-start(f32[2560,64]{1,0:T(8,128)} %get-tuple-element.84.cos_ref) | copy-start | bytes 1966084
  76.6 32.8 %copy-start.5 = (f32[1,128]{1,0:T(1,128)S(1)}, f32[1,128]{1,0:T(1,128)}, u32[]{:S(2)}) copy-start(f32[1,128]{1,0:T(1,128)} %add_bitcast_fusion.kg_ref) | copy-start | bytes 1540
  104.1 21.9 %all-to-all-start = ((bf16[64,8,512]{2,1,0:T(8,128)(2,1)}), bf16[64,8,512]{2,1,0:T(8,128)(2,1)S(1)}, u32[]{:S(2)}, u32[]{:S(2)}) async-start(bf16[64,8,512]{2,1,0:T(8,128)(2,1)} %bitcast.23), calls=%async_computation | async-start | bytes 1048576 | tf_op jit(solution)/shard_map/all_to_all | solution.py:463
  126.1 9.7 %collective-permute-start.3 = (bf16[64,512]{1,0:T(8,128)(2,1)S(1)}, bf16[64,512]{1,0:T(8,128)(2,1)S(1)}, u32[]{:S(2)}, u32[]{:S(2)}) collective-permute-start(bf16[64,512]{1,0:T(8,128)(2,1)S(1)} %dynamic-slice_bitcast_fusion), channel_id=1, source_target_pairs={{0,128},{128,0},{1,129},{129,1},{2,130},{130,2},{3,131},{131,3},{4... | collective-permute-start | bytes 196616 | tf_op jit(solution)/shard_map/ppermute | solution.py:24
  135.9 21.8 %copy-start.7 = (f32[512,512]{1,0:T(8,128)S(1)}, f32[512,512]{1,0:T(8,128)}, u32[]{:S(2)}) copy-start(f32[512,512]{1,0:T(8,128)} %get-tuple-element.59.rest_0_) | copy-start | bytes 3145732
  135.9 21.8 %copy-start.8 = (f32[512,512]{1,0:T(8,128)S(1)}, f32[512,512]{1,0:T(8,128)}, u32[]{:S(2)}) copy-start(f32[512,512]{1,0:T(8,128)} %get-tuple-element.60.rest_1_) | copy-start | bytes 3145732
  135.9 21.8 %copy-start.9 = (f32[512,512]{1,0:T(8,128)S(1)}, f32[512,512]{1,0:T(8,128)}, u32[]{:S(2)}) copy-start(f32[512,512]{1,0:T(8,128)} %get-tuple-element.61.rest_2_) | copy-start | bytes 3145732
  135.9 21.8 %copy-start.10 = (f32[512,512]{1,0:T(8,128)S(1)}, f32[512,512]{1,0:T(8,128)}, u32[]{:S(2)}) copy-start(f32[512,512]{1,0:T(8,128)} %get-tuple-element.62.rest_3_) | copy-start | bytes 3145732
  135.9 21.8 %copy-start.11 = (f32[512,512]{1,0:T(8,128)S(1)}, f32[512,512]{1,0:T(8,128)}, u32[]{:S(2)}) copy-start(f32[512,512]{1,0:T(8,128)} %get-tuple-element.63.rest_4_) | copy-start | bytes 3145732
  135.9 21.8 %copy-start.12 = (f32[512,512]{1,0:T(8,128)S(1)}, f32[512,512]{1,0:T(8,128)}, u32[]{:S(2)}) copy-start(f32[512,512]{1,0:T(8,128)} %get-tuple-element.64.rest_5_) | copy-start | bytes 3145732
  135.9 10.7 %collective-permute-start.4 = (bf16[128,512]{1,0:T(8,128)(2,1)S(1)}, bf16[128,512]{1,0:T(8,128)(2,1)S(1)}, u32[]{:S(2)}, u32[]{:S(2)}) collective-permute-start(bf16[128,512]{1,0:T(8,128)(2,1)S(1)} %pad_maximum_fusion.1), channel_id=1, source_target_pairs={{0,64},{16,80},{32,96},{48,112},{64,0},{80,16},{96,32},{112,48},{1... | collective-permute-start | bytes 393224 | tf_op jit(solution)/shard_map/ppermute | solution.py:28
  139.4 10.7 %collective-permute-start.5 = (bf16[128,512]{1,0:T(8,128)(2,1)S(1)}, bf16[128,512]{1,0:T(8,128)(2,1)S(1)}, u32[]{:S(2)}, u32[]{:S(2)}) collective-permute-start(bf16[128,512]{1,0:T(8,128)(2,1)S(1)} %pad_maximum_fusion.1), channel_id=1, source_target_pairs={{0,32},{16,48},{32,64},{48,80},{64,96},{80,112},{96,0},{112,16},{1... | collective-permute-start | bytes 393224 | tf_op jit(solution)/shard_map/ppermute | solution.py:28
  141.4 12.2 %collective-permute-start.6 = (bf16[128,512]{1,0:T(8,128)(2,1)S(1)}, bf16[128,512]{1,0:T(8,128)(2,1)S(1)}, u32[]{:S(2)}, u32[]{:S(2)}) collective-permute-start(bf16[128,512]{1,0:T(8,128)(2,1)S(1)} %pad_maximum_fusion.1), channel_id=1, source_target_pairs={{0,96},{16,112},{32,0},{48,16},{64,32},{80,48},{96,64},{112,80},{1... | collective-permute-start | bytes 393224 | tf_op jit(solution)/shard_map/ppermute | solution.py:28
  153.6 4.0 %collective-permute-start.9 = (bf16[512,512]{1,0:T(8,128)(2,1)S(1)}, bf16[512,512]{1,0:T(8,128)(2,1)S(1)}, u32[]{:S(2)}, u32[]{:S(2)}) collective-permute-start(bf16[512,512]{1,0:T(8,128)(2,1)S(1)} %constant_dynamic-update-slice_fusion.2.rest_9_), channel_id=1, source_target_pairs={{0,8},{8,0},{1,9},{9,1},{2,10},{10,2},{3,11},{11,3},{4,12},{12,4},... | collective-permute-start | bytes 1572872 | tf_op jit(solution)/shard_map/ppermute | solution.py:24
  155.0 10.6 %collective-permute-start.7 = (bf16[256,512]{1,0:T(8,128)(2,1)S(1)}, bf16[256,512]{1,0:T(8,128)(2,1)S(1)}, u32[]{:S(2)}, u32[]{:S(2)}) collective-permute-start(bf16[256,512]{1,0:T(8,128)(2,1)S(1)} %get-tuple-element.80), channel_id=1, source_target_pairs={{0,16},{16,32},{32,48},{48,64},{64,80},{80,96},{96,112},{112,0},{1... | collective-permute-start | bytes 786440 | tf_op jit(solution)/shard_map/ppermute | solution.py:28
  156.1 9.5 %collective-permute-start.8 = (bf16[256,512]{1,0:T(8,128)(2,1)S(1)}, bf16[256,512]{1,0:T(8,128)(2,1)S(1)}, u32[]{:S(2)}, u32[]{:S(2)}) collective-permute-start(bf16[256,512]{1,0:T(8,128)(2,1)S(1)} %get-tuple-element.80), channel_id=1, source_target_pairs={{0,112},{16,0},{32,16},{48,32},{64,48},{80,64},{96,80},{112,96},{1... | collective-permute-start | bytes 786440 | tf_op jit(solution)/shard_map/ppermute | solution.py:28
  165.7 5.7 %collective-permute-start.10 = (bf16[512,512]{1,0:T(8,128)(2,1)S(1)}, bf16[512,512]{1,0:T(8,128)(2,1)S(1)}, u32[]{:S(2)}, u32[]{:S(2)}) collective-permute-start(bf16[512,512]{1,0:T(8,128)(2,1)S(1)} %constant_dynamic-update-slice_fusion.6.rest_3_), channel_id=1, source_target_pairs={{0,8},{8,0},{1,9},{9,1},{2,10},{10,2},{3,11},{11,3},{4,12},{12,4},... | collective-permute-start | bytes 1572872 | tf_op jit(solution)/shard_map/ppermute | solution.py:24
  (7 other events, 56.1 us)
